TPU v7x, 32 devices: a whole 2x2x4 slice. The times are simulated.
32 devices in a mesh: rep: 8 (over y, x, core), fsdp: 4 (over z).
Axes of the slice: x: 2, y: 2, z: 4, core: 2. Of those that a mesh axis runs over, the one named last changes fastest.
Arguments:
- tokens: bfloat16 [4096, 4096], P('rep', 'fsdp'), may hold values from -6 to 6
- gate_weight: bfloat16 [4096, 7168], P('rep', 'fsdp'), may hold values from -0.09375 to 0.09375
- up_act: bfloat16 [4096, 7168], P('rep', 'fsdp'), may hold values from -6 to 6
- cotangent: bfloat16 [4096, 7168], P('rep', 'fsdp'), may hold values from -0.099609375 to 0.099609375
Outputs:
- grad_sum: bfloat16 [4096, 7168], P('rep', 'fsdp')
- curvature: float32 [7168], P('fsdp')
- spread: float32 [7168], P('fsdp')
All inputs are finite; a program needn't handle non-finite values.
Results may differ from a plain program's by a relative error of at most 0.024.
Values may be sent and summed in bfloat16 or wider, within the bound.
A program may use at most 128 MiB of HBM per device.

v0:
```python
import jax
import jax.numpy as jnp
from jax import lax
from jax.sharding import PartitionSpec as P


def shards(tokens, gate_weight, up_act, cotangent):
    features_all = lax.all_gather(tokens, "fsdp", axis=1, tiled=True)
    replicas = lax.axis_size("rep")

    def add_rows(block_rows):
        return jnp.dot(features_all, block_rows, preferred_element_type=jnp.float32)

    gate_pre = add_rows(lax.all_gather(gate_weight, "rep", axis=0, tiled=True))
    sigmoid_gate = jax.nn.sigmoid(gate_pre)
    deriv_one = sigmoid_gate * (1.0 + gate_pre * (1.0 - sigmoid_gate))
    deriv_two = sigmoid_gate * (1.0 - sigmoid_gate) * (2.0 + gate_pre * (1.0 - 2.0 * sigmoid_gate))
    weighted = cotangent.astype(jnp.float32) * up_act.astype(jnp.float32)
    token_coeff = (weighted * deriv_one).astype(jnp.bfloat16)
    bend_weight = weighted * deriv_two
    rep_grad = lax.dot_general(
        features_all, token_coeff, (((0,), (0,)), ((), ())), preferred_element_type=jnp.float32
    ).astype(jnp.bfloat16)
    own_proj = jnp.dot(features_all, rep_grad, preferred_element_type=jnp.float32)
    grad_shard = lax.psum_scatter(
        rep_grad.astype(jnp.float32).astype(jnp.bfloat16), "rep", scatter_dimension=0, tiled=True
    )
    mean_proj = add_rows(lax.all_gather(grad_shard, "rep", axis=0, tiled=True)) / replicas
    deviate = own_proj - mean_proj
    curv_part = jnp.sum(bend_weight * mean_proj * mean_proj, axis=0)
    spread_part = jnp.sum(bend_weight * deviate * deviate, axis=0)
    curvature, spread_total = lax.psum((curv_part, spread_part), "rep")
    return (grad_shard, curvature, spread_total / (replicas - 1))


def solution(mesh):
    placed = (P("rep", "fsdp"), P("rep", "fsdp"), P("rep", "fsdp"), P("rep", "fsdp"))
    return jax.shard_map(
        shards,
        mesh=mesh,
        in_specs=placed,
        out_specs=(P("rep", "fsdp"), P("fsdp"), P("fsdp")),
        check_vma=False,
    )
```

profile of v0, /device:TPU:0, one launch (start us, length us, event | category | flops | bytes accessed | tf_op | source)
XLA Modules:
  0.0 455.3 jit_solution(8435540799089013819)
XLA Ops:
  7.2 0.0 all-gather.4.cloned.1.call-start
  7.2 0.7 all-gather.4.cloned.1.call-update
  7.9 0.0 all-gather.6.cloned.1.call-start
  7.9 0.7 all-gather.6.cloned.1.call-update
  8.6 0.0 copy-start.2
  8.7 0.0 reduce-scatter.2.cloned.1.call-start
  8.7 84.3 %all-gather.4.cloned.1.call-done = bf16[512,4096]{1,0:T(8,128)(2,1)} async-done(((bf16[512,1024]{1,0:T(8,128)(2,1)}), bf16[512,4096]{1,0:T(8,128)(2,1)}) %all-gather.4.cloned.1.call-update) | async-done | bytes 4194320 | tf_op jit(solution)/shard_map/all_gather | solution.py:8
  93.0 81.3 %all-gather.6.cloned.1.call-done = bf16[4096,1792]{1,0:T(8,128)(2,1)} async-done(((bf16[512,1792]{1,0:T(8,128)(2,1)}), bf16[4096,1792]{1,0:T(8,128)(2,1)}) %all-gather.6.cloned.1.call-update) | async-done | bytes 14680080 | tf_op jit(solution)/shard_map/all_gather | solution.py:14
  174.3 0.0 copy-start
  174.3 0.0 copy-start.3
  174.3 16.7 %fusion.11 = f32[512,1792]{1,0:T(8,128)} fusion(bf16[512,4096]{1,0:T(8,128)(2,1)} %all-gather.4.cloned.1.call-done, bf16[4096,1792]{1,0:T(8,128)(2,1)} %all-gather.6.cloned.1.call-done), kind=kOutput, calls=%fused_computation.20 | convolution fusion | flops 7516192768 | bytes 22544384 | tf_op jit(solution)/shard_map/dot_general | solution.py:12
  191.0 0.0 copy-done.2
  191.0 0.0 copy-done
  191.0 0.0 copy-done.3
  191.0 15.3 %convolution_convert_fusion = bf16[1792,4096]{1,0:T(8,128)(2,1)} fusion(bf16[512,4096]{1,0:T(8,128)(2,1)S(1)} %copy-done, f32[512,1792]{1,0:T(8,128)} %fusion.11, bf16[512,1792]{1,0:T(8,128)(2,1)S(1)} %copy-done.2, bf16[512,1792]{1,0:T(8,128)(2,1)S(1)} %copy-done.3), kind=kOutput, calls=%fused_computation | convolution fusion | flops 7534542848 | bytes 26214400 | tf_op jit(solution)/shard_map/dot_general | solution.py:21
  206.3 0.0 reduce-scatter.2.cloned.1.call-update
  206.4 0.2 all-gather.8.cloned.1.call-start
  206.6 102.2 %reduce-scatter.2.cloned.1.call-done = bf16[512,1792]{0,1:T(8,128)(2,1)} async-done(((bf16[4096,1792]{0,1:T(8,128)(2,1)}), bf16[512,1792]{0,1:T(8,128)(2,1)}) %reduce-scatter.2.cloned.1.call-update) | async-done | bytes 1835024 | tf_op jit(solution)/shard_map/reduce_scatter | solution.py:25
  308.8 0.0 all-gather.8.cloned.1.call-update
  308.8 3.8 copy.7
  312.6 81.6 %all-gather.8.cloned.1.call-done = bf16[4096,1792]{0,1:T(8,128)(2,1)} async-done(((bf16[512,1792]{0,1:T(8,128)(2,1)}), bf16[4096,1792]{0,1:T(8,128)(2,1)}) %all-gather.8.cloned.1.call-update) | async-done | bytes 14680080 | tf_op jit(solution)/shard_map/all_gather | solution.py:28
  394.2 0.0 copy-start.1
  394.2 0.0 copy-start.4
  394.2 0.0 copy-start.5
  394.2 16.5 %fusion.6 = (f32[1792]{0:T(1024)S(1)}, f32[1792,512]{0,1:T(8,128)S(1)}) fusion(f32[512,1792]{1,0:T(8,128)} %fusion.11, bf16[512,1792]{1,0:T(8,128)(2,1)S(1)} %copy-done.2, bf16[512,1792]{1,0:T(8,128)(2,1)} %param.7, bf16[4096,1792]{0,1:T(8,128)(2,1)} %all-gather.8.cloned.1.call-done, bf16[512,4096]{1,0:T(8,128)(2,1)} %all-gather.4.cloned.1.call-done), kind=kOutput, calls=%fused_computation.11 | convolution fusion | flops 7532705792 | bytes 29891584 | tf_op jit(solution)/shard_map/dot_general | solution.py:12
  410.8 0.0 copy-done.1
  410.8 0.0 copy-done.4
  410.8 0.0 copy-done.5
  410.8 13.8 %fusion.7 = f32[1792]{0:T(1024)S(1)} fusion(f32[1792,512]{0,1:T(8,128)S(1)} %get-tuple-element.9, bf16[1792,4096]{1,0:T(8,128)(2,1)} %convolution_convert_fusion, bf16[512,4096]{1,0:T(8,128)(2,1)S(1)} %copy-done.1, f32[512,1792]{1,0:T(8,128)S(1)} %copy-done.5, bf16[512,1792]{1,0:T(8,128)(2,1)S(1)} %copy-done.2, bf16[512,1792]{1,0:T(8,128)(2,1)S(1)} %copy-done.4), kind=kOutput, calls=%fused_computation.12 | convolution fusion | flops 7532705792 | bytes 29891584 | tf_op jit(solution)/shard_map/dot_general | solution.py:24
  424.7 23.5 %all-reduce = (f32[1792]{0:T(1024)}, f32[1792]{0:T(1024)S(1)}) all-reduce(f32[1792]{0:T(1024)S(1)} %get-tuple-element.8, f32[1792]{0:T(1024)S(1)} %fusion.7), channel_id=1, replica_groups=mesh['rep'=8,'fsdp'=4] {'rep'}, use_global_device_ids=true, to_apply=%region_2.0 | all-reduce | flops 3584 | bytes 28672 | tf_op jit(solution)/shard_map/psum | solution.py:32
  448.1 0.6 broadcast_multiply_fusion
Async XLA Ops:
  7.2 85.9 %all-gather.4.cloned.1.call-start = ((), (), s32[]{:S(2)}) async-start(), calls=%async_computation.1 | async-start | bytes 5242880 | tf_op jit(solution)/shard_map/all_gather | solution.py:8
  7.9 166.4 %all-gather.6.cloned.1.call-start = ((), (), s32[]{:S(2)}) async-start(), calls=%async_computation.2 | async-start | bytes 16515072 | tf_op jit(solution)/shard_map/all_gather | solution.py:14
  8.6 182.4 %copy-start.2 = (bf16[512,1792]{1,0:T(8,128)(2,1)S(1)}, bf16[512,1792]{1,0:T(8,128)(2,1)}, u32[]{:S(2)}) copy-start(bf16[512,1792]{1,0:T(8,128)(2,1)} %param.6) | copy-start | bytes 5505028
  8.7 300.1 %reduce-scatter.2.cloned.1.call-start = ((), (), s32[]{:S(2)}) async-start(), calls=%async_computation.3 | async-start | bytes 16515072 | tf_op jit(solution)/shard_map/reduce_scatter | solution.py:25
  174.3 16.7 %copy-start = (bf16[512,4096]{1,0:T(8,128)(2,1)S(1)}, bf16[512,4096]{1,0:T(8,128)(2,1)}, u32[]{:S(2)}) copy-start(bf16[512,4096]{1,0:T(8,128)(2,1)} %all-gather.4.cloned.1.call-done) | copy-start | bytes 12582916
  174.3 16.7 %copy-start.3 = (bf16[512,1792]{1,0:T(8,128)(2,1)S(1)}, bf16[512,1792]{1,0:T(8,128)(2,1)}, u32[]{:S(2)}) copy-start(bf16[512,1792]{1,0:T(8,128)(2,1)} %param.7) | copy-start | bytes 5505028
  206.4 187.9 %all-gather.8.cloned.1.call-start = ((), (), s32[]{:S(2)}) async-start(), calls=%async_computation.4 | async-start | bytes 16515072 | tf_op jit(solution)/shard_map/all_gather | solution.py:28
  394.2 16.5 %copy-start.1 = (bf16[512,4096]{1,0:T(8,128)(2,1)S(1)}, bf16[512,4096]{1,0:T(8,128)(2,1)}, u32[]{:S(2)}) copy-start(bf16[512,4096]{1,0:T(8,128)(2,1)} %all-gather.4.cloned.1.call-done) | copy-start | bytes 12582916
  394.2 16.6 %copy-start.4 = (bf16[512,1792]{1,0:T(8,128)(2,1)S(1)}, bf16[512,1792]{1,0:T(8,128)(2,1)}, u32[]{:S(2)}) copy-start(bf16[512,1792]{1,0:T(8,128)(2,1)} %param.7) | copy-start | bytes 5505028
  394.2 16.6 %copy-start.5 = (f32[512,1792]{1,0:T(8,128)S(1)}, f32[512,1792]{1,0:T(8,128)}, u32[]{:S(2)}) copy-start(f32[512,1792]{1,0:T(8,128)} %fusion.11) | copy-start | bytes 11010052
Sparse Core Ops, SparseCore 0:
  9.5 83.4 all-gather.3
  94.9 79.3 all-gather.5
  206.5 102.2 reduce-scatter.1
  310.5 83.7 all-gather.7
where the time goes:
time: 456 us; the launch traced here: 455 us
  waiting for transfers between devices  351 us (77%)
  matrix products  62.4 us (14%)
  blocking collectives  23.5 us (5%)
  between operations  13.8 us (3%)
    reduce_scatter x1, waiting for transfers between devices, shards(): lax.psum_scatter(rep_grad.astype(jnp.float32).astype(jnp.bfloat16), 'rep'...  102 us
    all_gather x1, waiting for transfers between devices, shards(): features_all = lax.all_gather(tokens, 'fsdp', axis=1, tiled=True)  84.3 us
    all_gather x1, waiting for transfers between devices, shards(): lax.all_gather(grad_shard, 'rep', axis=0, tiled=True)  81.6 us
    all_gather x1, waiting for transfers between devices, shards(): gate_pre = add_rows(lax.all_gather(gate_weight, 'rep', axis=0, tiled=True))  81.3 us
    dot_general x2, matrix products, add_rows(): return jnp.dot(features_all, block_rows, preferred_element_type=jnp.float32)  33.2 us
    psum x1, blocking collectives, shards(): curvature, spread_total = lax.psum((curv_part, spread_part), 'rep')  23.5 us
    dot_general x1, matrix products, shards(): lax.dot_general(features_all, token_coeff, (((0,), (0,)), ((), ())), pref...  15.3 us
    dot_general x1, matrix products, shards(): jnp.dot(features_all, rep_grad, preferred_element_type=jnp.float32)  13.8 us
  transfers between devices with their start and end apart: 4, of which 4 were waited for; matrix products, arithmetic and copies ran while one was open for 1% of the time, Pallas kernels for 0%

commit v1 on v0

--- a/solution.py
+++ b/solution.py
@@ -5,7 +5,8 @@
 
 
 def shards(tokens, gate_weight, up_act, cotangent):
-    features_all = lax.all_gather(tokens, "fsdp", axis=1, tiled=True)
+    pieces = lax.all_gather(tokens, "fsdp", axis=0, tiled=False)
+    features_all = jnp.concatenate(pieces, axis=1)
     replicas = lax.axis_size("rep")
 
     def add_rows(block_rows):

time: 456 us -> 461 us (1.011)
  local copies, waits for them, and re-layouts: 3.83 us -> 10 us
  waiting for transfers between devices: 351 us -> 345 us
  matrix products: 62.4 us -> 67.6 us
    all_gather x1, waiting for transfers between devices: 81.3 us -> 75.1 us  [shards(): gate_pre = add_rows(lax.all_gather(gate_weight, 'rep', axis=0, tiled=True))]
    reshape x0 -> x1, local copies, waits for them, and re-layouts: none -> 6.21 us  [shards(): features_all = jnp.concatenate(pieces, axis=1)]
  transfers between devices with their start and end apart: 4 -> 4, of which waited for: 4 -> 4; matrix products, arithmetic and copies ran while one was open for 1% -> 2% of each run, Pallas kernels for 0% -> 0%
where the time goes in v1:
time: 461 us; the launch traced here: 460 us
  waiting for transfers between devices  345 us (75%)
  matrix products  67.6 us (15%)
  blocking collectives  23.5 us (5%)
  between operations  13.8 us (3%)
  local copies, waits for them, and re-layouts  10 us (2%)
    reduce_scatter x1, waiting for transfers between devices, shards(): lax.psum_scatter(rep_grad.astype(jnp.float32).astype(jnp.bfloat16), 'rep'...  102 us
    all_gather x1, waiting for transfers between devices, shards(): pieces = lax.all_gather(tokens, 'fsdp', axis=0, tiled=False)  84.3 us
    all_gather x1, waiting for transfers between devices, shards(): lax.all_gather(grad_shard, 'rep', axis=0, tiled=True)  81.7 us
    all_gather x1, waiting for transfers between devices, shards(): gate_pre = add_rows(lax.all_gather(gate_weight, 'rep', axis=0, tiled=True))  75.1 us
    dot_general x2, matrix products, add_rows(): return jnp.dot(features_all, block_rows, preferred_element_type=jnp.float32)  34.5 us
    psum x1, blocking collectives, shards(): curvature, spread_total = lax.psum((curv_part, spread_part), 'rep')  23.5 us
    dot_general x1, matrix products, shards(): jnp.dot(features_all, rep_grad, preferred_element_type=jnp.float32)  17 us
    dot_general x1, matrix products, shards(): lax.dot_general(features_all, token_coeff, (((0,), (0,)), ((), ())), pref...  16.2 us
  transfers between devices with their start and end apart: 4, of which 4 were waited for; matrix products, arithmetic and copies ran while one was open for 2% of the time, Pallas kernels for 0%

profile of v1, /device:TPU:0, one launch (start us, length us, event | category | flops | bytes accessed | tf_op | source)
XLA Modules:
  0.0 460.4 jit_solution(15194610680115751713)
XLA Ops:
  7.2 0.0 all-gather.9.cloned.1.call-start
  7.2 0.7 all-gather.9.cloned.1.call-update
  7.9 0.0 all-gather.5.cloned.1.call-start
  7.9 0.7 all-gather.5.cloned.1.call-update
  8.6 0.0 reduce-scatter.2.cloned.1.call-start
  8.7 84.3 %all-gather.9.cloned.1.call-done = bf16[2048,1024]{1,0:T(8,128)(2,1)} async-done(((bf16[512,1024]{1,0:T(8,128)(2,1)}), bf16[2048,1024]{1,0:T(8,128)(2,1)}) %all-gather.9.cloned.1.call-update) | async-done | bytes 4194320 | tf_op jit(solution)/shard_map/all_gather | solution.py:8
  93.0 6.2 %copy.9 = bf16[512,4,1024]{0,2,1:T(8,128)(2,1)} copy(bf16[512,4,1024]{2,0,1:T(8,128)(2,1)} %bitcast.24) | data formatting | bytes 8388608 | tf_op jit(solution)/shard_map/reshape | solution.py:9
  99.2 75.1 %all-gather.5.cloned.1.call-done = bf16[4096,1792]{1,0:T(8,128)(2,1)} async-done(((bf16[512,1792]{1,0:T(8,128)(2,1)}), bf16[4096,1792]{1,0:T(8,128)(2,1)}) %all-gather.5.cloned.1.call-update) | async-done | bytes 14680080 | tf_op jit(solution)/shard_map/all_gather | solution.py:15
  174.3 0.0 copy-start
  174.3 0.0 copy-start.1
  174.3 16.6 %fusion.11 = f32[512,1792]{1,0:T(8,128)} fusion(bf16[512,4096]{0,1:T(8,128)(2,1)} %bitcast.20, bf16[4096,1792]{1,0:T(8,128)(2,1)} %all-gather.5.cloned.1.call-done), kind=kOutput, calls=%fused_computation.20 | convolution fusion | flops 7516192768 | bytes 22544384 | tf_op jit(solution)/shard_map/dot_general | solution.py:13
  191.0 0.0 copy-done
  191.0 0.0 copy-done.1
  191.0 16.2 %convolution_convert_fusion = bf16[1792,4096]{1,0:T(8,128)(2,1)} fusion(bf16[512,4096]{0,1:T(8,128)(2,1)S(1)} %bitcast.23, f32[512,1792]{1,0:T(8,128)} %fusion.11, bf16[512,1792]{1,0:T(8,128)(2,1)S(1)} %copy-done.1, bf16[512,1792]{1,0:T(8,128)(2,1)} %param.7), kind=kOutput, calls=%fused_computation | convolution fusion | flops 7534542848 | bytes 26214400 | tf_op jit(solution)/shard_map/dot_general | solution.py:22
  207.2 0.0 reduce-scatter.2.cloned.1.call-update
  207.2 0.2 all-gather.7.cloned.1.call-start
  207.4 102.1 %reduce-scatter.2.cloned.1.call-done = bf16[512,1792]{0,1:T(8,128)(2,1)} async-done(((bf16[4096,1792]{0,1:T(8,128)(2,1)}), bf16[512,1792]{0,1:T(8,128)(2,1)}) %reduce-scatter.2.cloned.1.call-update) | async-done | bytes 1835024 | tf_op jit(solution)/shard_map/reduce_scatter | solution.py:26
  309.5 0.0 all-gather.7.cloned.1.call-update
  309.6 3.8 copy.10
  313.4 81.7 %all-gather.7.cloned.1.call-done = bf16[4096,1792]{0,1:T(8,128)(2,1)} async-done(((bf16[512,1792]{0,1:T(8,128)(2,1)}), bf16[4096,1792]{0,1:T(8,128)(2,1)}) %all-gather.7.cloned.1.call-update) | async-done | bytes 14680080 | tf_op jit(solution)/shard_map/all_gather | solution.py:29
  395.0 17.8 %fusion.6 = (f32[1792]{0:T(1024)S(1)}, f32[1792,512]{0,1:T(8,128)}) fusion(f32[512,1792]{1,0:T(8,128)} %fusion.11, bf16[512,1792]{1,0:T(8,128)(2,1)S(1)} %copy-done.1, bf16[512,1792]{1,0:T(8,128)(2,1)} %param.7, bf16[4096,1792]{0,1:T(8,128)(2,1)} %all-gather.7.cloned.1.call-done, bf16[512,4096]{0,1:T(8,128)(2,1)} %bitcast.21), kind=kOutput, calls=%fused_computation.11 | convolution fusion | flops 7532705792 | bytes 29891584 | tf_op jit(solution)/shard_map/dot_general | solution.py:13
  412.8 17.0 %fusion.7 = f32[1792]{0:T(1024)S(1)} fusion(f32[1792,512]{0,1:T(8,128)} %get-tuple-element.15, bf16[1792,4096]{1,0:T(8,128)(2,1)} %convolution_convert_fusion, bf16[512,4096]{0,1:T(8,128)(2,1)} %bitcast.22, f32[512,1792]{1,0:T(8,128)} %fusion.11, bf16[512,1792]{1,0:T(8,128)(2,1)S(1)} %copy-done.1, bf16[512,1792]{1,0:T(8,128)(2,1)} %param.7), kind=kOutput, calls=%fused_computation.12 | convolution fusion | flops 7532705792 | bytes 29891584 | tf_op jit(solution)/shard_map/dot_general | solution.py:25
  429.8 23.5 %all-reduce = (f32[1792]{0:T(1024)}, f32[1792]{0:T(1024)S(1)}) all-reduce(f32[1792]{0:T(1024)S(1)} %get-tuple-element.14, f32[1792]{0:T(1024)S(1)} %fusion.7), channel_id=1, replica_groups=mesh['rep'=8,'fsdp'=4] {'rep'}, use_global_device_ids=true, to_apply=%region_2.0 | all-reduce | flops 3584 | bytes 28672 | tf_op jit(solution)/shard_map/psum | solution.py:33
  453.3 0.6 broadcast_multiply_fusion
Async XLA Ops:
  7.2 85.9 %all-gather.9.cloned.1.call-start = ((), (), s32[]{:S(2)}) async-start(), calls=%async_computation.4 | async-start | bytes 5242880 | tf_op jit(solution)/shard_map/all_gather | solution.py:8
  7.9 166.4 %all-gather.5.cloned.1.call-start = ((), (), s32[]{:S(2)}) async-start(), calls=%async_computation.1 | async-start | bytes 16515072 | tf_op jit(solution)/shard_map/all_gather | solution.py:15
  8.6 300.9 %reduce-scatter.2.cloned.1.call-start = ((), (), s32[]{:S(2)}) async-start(), calls=%async_computation.2 | async-start | bytes 16515072 | tf_op jit(solution)/shard_map/reduce_scatter | solution.py:26
  174.3 16.6 %copy-start = (bf16[512,4,1024]{0,2,1:T(8,128)(2,1)S(1)}, bf16[512,4,1024]{0,2,1:T(8,128)(2,1)}, u32[]{:S(2)}) copy-start(bf16[512,4,1024]{0,2,1:T(8,128)(2,1)} %copy.9) | copy-start | bytes 12582916
  174.3 16.6 %copy-start.1 = (bf16[512,1792]{1,0:T(8,128)(2,1)S(1)}, bf16[512,1792]{1,0:T(8,128)(2,1)}, u32[]{:S(2)}) copy-start(bf16[512,1792]{1,0:T(8,128)(2,1)} %param.6) | copy-start | bytes 5505028
  207.2 187.8 %all-gather.7.cloned.1.call-start = ((), (), s32[]{:S(2)}) async-start(), calls=%async_computation.3 | async-start | bytes 16515072 | tf_op jit(solution)/shard_map/all_gather | solution.py:29
Sparse Core Ops, SparseCore 0:
  9.5 83.4 all-gather.8
  94.9 79.3 all-gather.4
  207.3 102.1 reduce-scatter.1
  311.3 83.7 all-gather.6
